TPU v7x, 256 devices: a whole 4x4x8 slice. The times are simulated.
256 devices in a mesh: ctx: 16 (over z_lo, y, core), pb: 16 (over x, z_hi).
Axes of the slice: x: 4, y: 4, z: 8 (z_hi: 4, z_lo: 2; z = z_hi * 2 + z_lo), core: 2. Of those that a mesh axis runs over, the one named last changes fastest.
Arguments:
- queries: bfloat16 [256, 64, 8, 128], P('pb'), may hold values from -6 to 6
- keys: bfloat16 [16384, 128], P('ctx'), may hold values from -6 to 6
- values: bfloat16 [16384, 128], P('ctx'), may hold values from -6 to 6
- outputs_saved: bfloat16 [256, 64, 8, 128], P('pb'), may hold values from -6 to 6
- grad_out: bfloat16 [256, 64, 8, 128], P('pb'), may hold values from -6 to 6
- saved_lse: float32 [256, 64, 8], P('pb'), may hold values from 7 to 9
- block_lists: int32 [256, 96], P('pb'), may hold values from -1 to 127, as said below
Outputs:
- query_grad: float32 [256, 64, 8, 128], P('pb', 'ctx')
- key_grad: float32 [16384, 128], P(('ctx', 'pb'))
- value_grad: float32 [16384, 128], P(('ctx', 'pb'))
Inputs may be any that keep to these rules, and one draw needn't show every extreme that they name: `block_lists`: each row lists distinct blocks in rising order, then -1 in the remaining entries. Of one row's blocks at most 6 lie in one run of 8 blocks (j * 8 to j * 8 + 7), and in every row exactly 6 lie in some such run.
All inputs are finite; a program needn't handle non-finite values.
Results may differ from a plain program's by a relative error of at most 0.0029.
Values sent between devices are 32-bit elements; how exact they have to be, the bound alone decides.
A program may use at most 128 MiB of HBM per device.

v0:
```python
from functools import partial

import jax
import jax.numpy as jnp
from jax import lax
from jax.sharding import PartitionSpec as P

BLK = 128
CAP = 6
BLK_DEV = 8


def slot_table(block_lists, local_blocks, shard_index, slot_count):
    first_block = shard_index * local_blocks
    offset = block_lists - first_block
    inside = (block_lists >= 0) & (offset >= 0) & (offset < local_blocks)
    blocks = jnp.arange(local_blocks, dtype=jnp.int32)
    member = jnp.any(inside[:, :, None] & (offset[:, :, None] == blocks[None, None, :]), axis=1)
    position = jnp.cumsum(member.astype(jnp.int32), axis=1) - 1
    wanted = jnp.arange(slot_count, dtype=jnp.int32)
    slot_hit = member[:, None, :] & (position[:, None, :] == wanted[None, :, None])
    chosen = jnp.sum(slot_hit.astype(jnp.int32) * blocks[None, None, :], axis=2)
    live_slots = jnp.any(slot_hit, axis=2)
    return (chosen, live_slots)


def tile_terms(q_rows, dout_rows, lse_rows, delta_rows, key_slab, value_slab, live_cols, factor):
    scores = factor * jnp.einsum("rd,kd->rk", q_rows, key_slab, preferred_element_type=jnp.float32)
    prob_tile = jnp.where(live_cols[None, :], jnp.exp(scores - lse_rows[:, None]), 0.0)
    dprob_tile = jnp.einsum("rd,kd->rk", dout_rows, value_slab, preferred_element_type=jnp.float32)
    dscore = (prob_tile * (dprob_tile - delta_rows[:, None])).astype(jnp.bfloat16)
    return (prob_tile, dscore)


def question_step(keep_rows, factor, carry, element):
    q_all, dout_all, lse_all, delta_all, slab_k, slab_v, cols = element
    head_width = q_all.shape[-1]
    q_rows = q_all.reshape(-1, head_width)
    dout_rows = dout_all.reshape(-1, head_width)
    prob_tile, dscore = tile_terms(
        q_rows, dout_rows, lse_all.reshape(-1), delta_all.reshape(-1), slab_k, slab_v, cols, factor
    )
    key_part = factor * jnp.einsum("rk,rd->kd", dscore, q_rows, preferred_element_type=jnp.float32)
    value_part = jnp.einsum(
        "rk,rd->kd", prob_tile.astype(jnp.bfloat16), dout_rows, preferred_element_type=jnp.float32
    )
    query_part = factor * jnp.dot(dscore, slab_k, preferred_element_type=jnp.float32)
    return (carry, (key_part, value_part, query_part.reshape(q_all.shape)))


def local(queries, keys, values, outputs_saved, grad_out, saved_lse, block_lists):
    head_width = queries.shape[-1]
    factor = head_width ** (-0.5)
    local_blocks = BLK_DEV
    block_rows = BLK
    slot_count = CAP
    key_blocks = keys.reshape(local_blocks, block_rows, head_width)
    value_blocks = values.reshape(local_blocks, block_rows, head_width)
    shard_index = lax.axis_index("ctx")
    chosen, live_slots = slot_table(block_lists, local_blocks, shard_index, slot_count)
    question_count = chosen.shape[0]
    key_slab = key_blocks[chosen].reshape(question_count, slot_count * block_rows, head_width)
    value_slab = value_blocks[chosen].reshape(question_count, slot_count * block_rows, head_width)
    live_cols = jnp.repeat(live_slots, block_rows, axis=1)
    row_delta = jnp.sum(grad_out.astype(jnp.float32) * outputs_saved.astype(jnp.float32), axis=-1)
    scanned = (queries, grad_out, saved_lse, row_delta, key_slab, value_slab, live_cols)
    stepper = partial(question_step, True, factor)
    unused_carry, (key_parts, value_parts, query_part) = lax.scan(stepper, 0, scanned)
    flat_chosen = chosen.reshape(-1)
    zero_acc = jnp.zeros((local_blocks, block_rows, head_width), jnp.float32)
    key_acc = zero_acc.at[flat_chosen].add(key_parts.reshape(-1, block_rows, head_width))
    value_acc = zero_acc.at[flat_chosen].add(value_parts.reshape(-1, block_rows, head_width))
    key_grad, value_grad = (
        lax.psum_scatter(key_acc.reshape(-1, head_width), "pb", scatter_dimension=0, tiled=True),
        lax.psum_scatter(value_acc.reshape(-1, head_width), "pb", scatter_dimension=0, tiled=True),
    )
    query_grad = lax.psum_scatter(query_part, "ctx", scatter_dimension=1, tiled=True)
    return (query_grad, key_grad, value_grad)


def solution(mesh):
    placed = (
        P("pb", None, None, None),
        P("ctx", None),
        P("ctx", None),
        P("pb", None, None, None),
        P("pb", None, None, None),
        P("pb", None, None),
        P("pb", None),
    )
    return jax.shard_map(
        local,
        mesh=mesh,
        in_specs=placed,
        out_specs=(P("pb", "ctx", None, None), P(("ctx", "pb"), None), P(("ctx", "pb"), None)),
        check_vma=False,
    )
```

profile of v0, /device:TPU:8, one launch (start us, length us, event | category | flops | bytes accessed | tf_op | source)
XLA Modules:
  0.0 378.4 jit_solution(1000595876576324041)
XLA Ops:
  10.5 2.8 gather_fusion.1
  13.3 2.7 gather_fusion
  16.2 2.8 multiply_reduce_fusion
  19.0 159.6 %while.14 = (s32[]{:T(128)}, f32[16,768,128]{2,1,0:T(8,128)}, f32[16,768,128]{2,1,0:T(8,128)}, f32[16,64,8,128]{3,2,1,0:T(8,128)}, pred[16,768]{1,0:T(8,128)(4,1...) while((s32[]{:T(128)}, f32[16,768,128]{2,1,0:T(8,128)}, ...), condition=%wide.region_6.7_spmd, body=%wide.region_5.6_spmd.sunk | while | flops 506232832 | bytes 9272705 | solution.py:68
  22.8 2.1 fusion.55
  24.9 2.1 fusion.56
  32.8 2.1 fusion.55
  34.9 2.1 fusion.56
  36.9 2.0 fusion.57
  42.8 2.1 fusion.55
  44.8 2.1 fusion.56
  46.9 2.0 fusion.57
  52.7 2.1 fusion.55
  54.8 2.1 fusion.56
  62.7 2.1 fusion.55
  64.8 2.1 fusion.56
  72.7 2.1 fusion.55
  74.7 2.1 fusion.56
  82.7 2.1 fusion.55
  84.7 2.1 fusion.56
  92.6 2.1 fusion.55
  94.7 2.1 fusion.56
  96.8 2.0 fusion.57
  102.6 2.1 fusion.55
  104.7 2.1 fusion.56
  106.8 2.0 fusion.57
  112.6 2.1 fusion.55
  114.6 2.1 fusion.56
  116.7 2.0 fusion.57
  122.6 2.1 fusion.55
  124.6 2.1 fusion.56
  126.7 2.0 fusion.57
  132.5 2.1 fusion.55
  134.6 2.1 fusion.56
  142.5 2.1 fusion.55
  144.6 2.1 fusion.56
  152.5 2.1 fusion.55
  154.6 2.1 fusion.56
  156.6 2.0 fusion.57
  162.5 2.1 fusion.55
  164.5 2.1 fusion.56
  172.4 2.1 fusion.55
  174.5 2.1 fusion.56
  176.6 2.0 fusion.57
  178.9 12.9 %scatter_fusion = f32[8,128,128]{2,1,0:T(8,128)S(1)} fusion(f32[8,128,128]{2,1,0:T(8,128)S(1)} %broadcast_in_dim.48.clone, s32[96]{0:T(128)S(1)} %fusion.29, f32[96,128,128]{2,1,0:T(8,128)} %bitcast.85), kind=kCustom, calls=%fused_computation.2 | custom fusion | flops 1572864 | bytes 18874752 | tf_op jit(solution)/shard_map/scatter-add | solution.py:71
  192.7 13.0 %scatter_fusion.1 = f32[8,128,128]{2,1,0:T(8,128)S(1)} fusion(f32[8,128,128]{2,1,0:T(8,128)S(1)} %broadcast_in_dim.48.clone.1, s32[96]{0:T(128)S(1)} %fusion.29, f32[96,128,128]{2,1,0:T(8,128)} %bitcast.86), kind=kCustom, calls=%fused_computation.3 | custom fusion | flops 1572864 | bytes 18874752 | tf_op jit(solution)/shard_map/scatter-add | solution.py:72
  207.8 106.4 %all-reduce.3.cloned.1.call-done = f32[16,64,8,128]{3,2,1,0:T(8,128)} async-done(((f32[16,64,8,128]{3,2,1,0:T(8,128)}), f32[16,64,8,128]{3,2,1,0:T(8,128)}) %all-reduce.3.cloned.1.call-update) | async-done | bytes 4194320
  315.8 55.2 %reduce-scatter.8.cloned.1.call-done = f32[64,128]{1,0:T(8,128)} async-done(((f32[1024,128]{1,0:T(8,128)}), f32[64,128]{1,0:T(8,128)}) %reduce-scatter.8.cloned.1.call-update) | async-done | bytes 32784 | tf_op jit(solution)/shard_map/reduce_scatter | solution.py:75
  (182 shorter events, 83.8 us)
Async XLA Ops:
  8.0 2.5 copy-start
  8.0 306.1 %all-reduce.3.cloned.1.call-start = ((), (), s32[]{:S(2)}) async-start(), calls=%async_computation.4 | async-start | bytes 8388608
  10.5 2.8 copy-start.3
  13.3 2.9 copy-start.4
  178.6 137.2 %reduce-scatter.6.cloned.1.call-start = ((), (), s32[]{:S(2)}) async-start(), calls=%async_computation.2 | async-start | bytes 557056 | tf_op jit(solution)/shard_map/reduce_scatter | solution.py:74
  191.8 0.8 copy-start.2
  192.6 178.4 %reduce-scatter.8.cloned.1.call-start = ((), (), s32[]{:S(2)}) async-start(), calls=%async_computation.3 | async-start | bytes 557056 | tf_op jit(solution)/shard_map/reduce_scatter | solution.py:75
  192.7 13.8 %copy-start.5 = (u32[256]{0:T(256)S(1)}, u32[256]{0:T(256)}, u32[]{:S(2)}) copy-start(u32[256]{0:T(256)} %constant.58) | copy-start | bytes 3076
  205.7 0.8 copy-start.1
Sparse Core Ops, SparseCore 0:
  178.7 135.3 all-reduce.2
Sparse Core Ops, SparseCore 1:
  192.7 89.8 reduce-scatter.5
  286.5 84.5 reduce-scatter.7
where the time goes:
time: 381 us; the launch traced here: 378 us
  waiting for transfers between devices  162 us (43%)
  matrix products  143 us (38%)
  other arithmetic  30.7 us (8%)
  local copies, waits for them, and re-layouts  26 us (7%)
  between operations  16.3 us (4%)
    unnamed x4, waiting for transfers between devices  106 us
    reduce_scatter x1, waiting for transfers between devices, local(): lax.psum_scatter(value_acc.reshape(-1, head_width), 'pb', scatter_dimensi...  55.2 us
    dot_general x16, matrix products, question_step(): jnp.einsum('rk,rd->kd', prob_tile.astype(jnp.bfloat16), dout_rows, prefer...  33.1 us
    dot_general x16, matrix products, question_step(): jnp.einsum('rk,rd->kd', dscore, q_rows, preferred_element_type=jnp.float32)  33.1 us
    dot_general x16, matrix products, question_step(): jnp.dot(dscore, slab_k, preferred_element_type=jnp.float32)  32 us
    dot_general x16, matrix products, tile_terms(): jnp.einsum('rd,kd->rk', q_rows, key_slab, preferred_element_type=jnp.floa...  23.2 us
    dot_general x16, matrix products, tile_terms(): jnp.einsum('rd,kd->rk', dout_rows, value_slab, preferred_element_type=jnp...  21.8 us
    dynamic_slice x64, local copies, waits for them, and re-layouts, local(): lax.scan(stepper, 0, scanned)  13 us
  transfers between devices with their start and end apart: 3, of which 2 were waited for; matrix products, arithmetic and copies ran while one was open for 8% of the time, Pallas kernels for 0%

commit v1 on v0

v1 whole, which is shorter than its diff:
```python
from functools import partial

import jax
import jax.numpy as jnp
from jax import lax
from jax.experimental import pallas as pl
from jax.experimental.pallas import tpu as pltpu
from jax.sharding import PartitionSpec as P

BLK = 128
CAP = 6
BLK_DEV = 8
D = 128
MESH = pl.DeviceIdType.MESH

NT = (((1,), (1,)), ((), ()))
NN = (((1,), (0,)), ((), ()))


def dot(a, b, dims):
    return lax.dot_general(a, b, dims, preferred_element_type=jnp.float32)


def tiles_kernel(per_step, rows, lists_ref, q_ref, do_ref, o_ref, lse_ref, k_ref, v_ref,
                 qg_ref, kv_ref, kt_ref, delta_ref, acc_ref):
    factor = D ** -0.5
    step = pl.program_id(0)
    first = lax.axis_index("ctx") * BLK_DEV
    width = lists_ref.shape[1]
    dests = qg_ref.shape[0]
    part = rows // dests

    @pl.when(step == 0)
    def _():
        kv_ref[...] = jnp.zeros_like(kv_ref)
        for b in range(BLK_DEV):
            kt_ref[b] = k_ref[pl.ds(b * BLK, BLK), :].T

    ones = jnp.ones((8, 2 * D), jnp.bfloat16)

    def question(local, _):
        row = step * per_step + local
        prod = do_ref[local].astype(jnp.float32) * o_ref[local].astype(jnp.float32)
        high = prod.astype(jnp.bfloat16)
        low = (prod - high.astype(jnp.float32)).astype(jnp.bfloat16)
        delta_ref[...] = dot(ones, jnp.concatenate([high, low], axis=1), NT)
        acc_ref[...] = jnp.zeros_like(acc_ref)

        def probe(_, span):
            low_end, high_end = span
            mid = (low_end + high_end) // 2
            entry = lists_ref[row, jnp.minimum(mid, width - 1)]
            less = (entry >= 0) & (entry < first) & (mid < high_end)
            return jnp.where(less, mid + 1, low_end), jnp.where(less, high_end, mid)

        start, _ = lax.fori_loop(0, 7, probe, (jnp.int32(0), jnp.int32(width)), unroll=True)
        block_of = []
        count = jnp.int32(0)
        for j in range(CAP):
            at = start + j
            entry = lists_ref[row, jnp.minimum(at, width - 1)] - first
            inside = (at < width) & (entry >= 0) & (entry < BLK_DEV)
            count = count + inside.astype(jnp.int32)
            block_of.append(jnp.clip(entry, 0, BLK_DEV - 1))

        def tile(blocks):
            q = q_ref[local]
            do = do_ref[local]
            kb = jnp.concatenate([k_ref[pl.ds(pl.multiple_of(b * BLK, BLK), BLK), :] for b in blocks], axis=0)
            vb = jnp.concatenate([v_ref[pl.ds(pl.multiple_of(b * BLK, BLK), BLK), :] for b in blocks], axis=0)
            kt = jnp.concatenate([kt_ref[b] for b in blocks], axis=1)
            prob = jnp.exp(dot(kb, q, NT) * factor - lse_ref[local])
            dprob = dot(vb, do, NT)
            dscore = (prob * (dprob - delta_ref[0:1, :])).astype(jnp.bfloat16)
            value_part = dot(prob.astype(jnp.bfloat16), do, NN)
            key_part = dot(dscore, q, NN) * factor
            acc_ref[...] += dot(kt, dscore, NN)
            for j, b in enumerate(blocks):
                for h in range(2):
                    piece = slice(j * BLK + h * (BLK // 2), j * BLK + (h + 1) * (BLK // 2))
                    kv_ref[2 * b + h, 0] += key_part[piece]
                    kv_ref[2 * b + h, 1] += value_part[piece]

        for j in range(0, CAP, 2):
            @pl.when(count >= j + 2)
            def _():
                tile([block_of[j], block_of[j + 1]])

            @pl.when(count == j + 1)
            def _():
                tile([block_of[j]])

        grad = acc_ref[...].T * factor
        for s in range(dests):
            z, y, c = s // 8, (s // 2) % 4, s % 2
            qg_ref[c * 8 + z * 4 + y, local] = grad[s * part:(s + 1) * part]
        return 0

    lax.fori_loop(0, per_step, question, 0)


def tiles(queries, keys, values, outputs_saved, grad_out, saved_lse, block_lists, dests, groups, per_step):
    questions, qlen, heads, width = queries.shape
    rows = qlen * heads
    part = rows // dests
    flat = lambda a: a.reshape(questions, rows, width)
    block = pl.BlockSpec((per_step, rows, width), lambda i: (i, 0, 0))
    whole = pl.BlockSpec(keys.shape, lambda i: (0, 0))
    return pl.pallas_call(
        partial(tiles_kernel, per_step, rows),
        grid=(questions // per_step,),
        in_specs=[
            pl.BlockSpec(memory_space=pltpu.SMEM),
            block, block, block,
            pl.BlockSpec((per_step, 1, rows), lambda i: (i, 0, 0)),
            whole, whole,
        ],
        out_specs=[
            pl.BlockSpec((dests, per_step, part, width), lambda i: (0, i, 0, 0)),
            pl.BlockSpec((groups, 2, keys.shape[0] // groups, width), lambda i: (0, 0, 0, 0)),
        ],
        out_shape=[
            jax.ShapeDtypeStruct((dests, questions, part, width), jnp.float32),
            jax.ShapeDtypeStruct((groups, 2, keys.shape[0] // groups, width), jnp.float32),
        ],
        scratch_shapes=[
            pltpu.VMEM((BLK_DEV, width, BLK), jnp.bfloat16),
            pltpu.VMEM((8, rows), jnp.float32),
            pltpu.VMEM((width, rows), jnp.float32),
        ],
        compiler_params=pltpu.CompilerParams(dimension_semantics=("arbitrary",)),
        name="tiles",
    )(block_lists, flat(queries), flat(grad_out), flat(outputs_saved),
      saved_lse.reshape(questions, 1, rows), keys, values)


def reduce_kernel(pieces, qp_ref, kv_ref, qout_ref, kout_ref, vout_ref,
                  acc, other, relay_l, relay_r, from_l, from_r, from_z,
                  kacc, krelay_l, krelay_r, kfrom_l, kfrom_r, kfrom_z,
                  load_sem, send_sem, recv_sem, ksend_sem, krecv_sem):
    ctx, pb = lax.axis_index("ctx"), lax.axis_index("pb")
    c, y, z = ctx % 2, (ctx // 2) % 4, ctx // 8
    x, w = pb // 4, pb % 4
    yn, yp, yo = (y + 1) % 4, (y + 3) % 4, (y + 2) % 4
    xn, xp, xo = (x + 1) % 4, (x + 3) % 4, (x + 2) % 4
    at_ctx = lambda z_, y_, c_: {"ctx": z_ * 8 + y_ * 2 + c_}
    at_pb = lambda x_, w_: {"pb": x_ * 4 + w_}
    mate, right, left, across = at_ctx(z, y, 1 - c), at_ctx(z, yn, c), at_ctx(z, yp, c), at_ctx(1 - z, y, c)
    kright, kleft = at_pb(xn, w), at_pb(xp, w)
    kfar = [at_pb(x, (w + d) % 4) for d in (1, 2, 3)]
    n = qp_ref.shape[3] // pieces
    h = n // 2

    loads = [
        pltpu.make_async_copy(qp_ref.at[c, :, :, pl.ds(p * n, n)], acc.at[:, :, pl.ds(p * n, n)], load_sem.at[p])
        for p in range(pieces)
    ]
    kload = pltpu.make_async_copy(kv_ref, kacc, load_sem.at[pieces])
    for copy in loads + [kload]:
        copy.start()

    barrier = pltpu.get_barrier_semaphore()
    partners = [mate, right, left, across, kright, kleft] + kfar
    for device in partners:
        pl.semaphore_signal(barrier, inc=1, device_id=device, device_id_type=MESH)
    pl.semaphore_wait(barrier, len(partners))

    def remote(src, dst, sems, at, device):
        return pltpu.make_async_remote_copy(
            src_ref=src, dst_ref=dst, send_sem=sems[0].at[at], recv_sem=sems[1].at[at],
            device_id=device, device_id_type=MESH)

    qsems, ksems = (send_sem, recv_sem), (ksend_sem, krecv_sem)
    copies = {}
    for p in range(pieces):
        every, one, two = pl.ds(p * n, n), pl.ds(p * n, h), pl.ds(p * n + h, h)
        make = lambda k, src, dst, device: remote(src, dst, qsems, p * 8 + k, device)
        copies[p] = [
            make(0, qp_ref.at[1 - c, :, :, every], other.at[:, :, every], mate),
            make(1, acc.at[:, yo, one], relay_l.at[p], right),
            make(2, acc.at[:, yo, two], relay_r.at[p], left),
            make(3, acc.at[:, yn, two], from_l.at[p, 1], right),
            make(4, acc.at[:, yp, one], from_r.at[p, 0], left),
            make(5, acc.at[:, yn, one], from_l.at[p, 0], right),
            make(6, acc.at[:, yp, two], from_r.at[p, 1], left),
            make(7, acc.at[1 - z, y, every], from_z.at[p], across),
        ]
    one, two = pl.ds(0, 2), pl.ds(2, 2)
    make = lambda k, src, dst, device: remote(src, dst, ksems, k, device)
    kcopies = [
        make(0, kv_ref.at[xo, one], krelay_l, kright),
        make(1, kv_ref.at[xo, two], krelay_r, kleft),
        make(2, kv_ref.at[xn, two], kfrom_l.at[1], kright),
        make(3, kv_ref.at[xp, one], kfrom_r.at[0], kleft),
        make(4, kacc.at[xn, one], kfrom_l.at[0], kright),
        make(5, kacc.at[xp, two], kfrom_r.at[1], kleft),
    ] + [make(6 + i, kacc.at[x, (w + i + 1) % 4], kfrom_z.at[i], kfar[i]) for i in range(3)]

    for p in range(pieces):
        copies[p][0].start()
        if p == 0:
            for copy in kcopies[:4]:
                copy.start()

    def mated(p):
        every = pl.ds(p * n, n)
        loads[p].wait()
        copies[p][0].wait_recv()
        acc[:, :, every] += other[:, :, every]
        for copy in copies[p][1:5]:
            copy.start()

    def relayed(p):
        one, two = pl.ds(p * n, h), pl.ds(p * n + h, h)
        copies[p][1].wait_recv()
        acc[:, yn, one] += relay_l[p]
        copies[p][5].start()
        copies[p][2].wait_recv()
        acc[:, yp, two] += relay_r[p]
        copies[p][6].start()

    def joined(p):
        for copy in copies[p][3:7]:
            copy.wait_recv()
        for i in range(2):
            part = pl.ds(p * n + i * h, h)
            acc[:, y, part] += from_l[p, i] + from_r[p, i]
        copies[p][7].start()

    def finished(p):
        every = pl.ds(p * n, n)
        copies[p][7].wait_recv()
        qout_ref[every] = acc[z, y, every] + from_z[p]

    def krelayed():
        kload.wait()
        kcopies[0].wait_recv()
        kacc[xn, one] += krelay_l[...]
        kcopies[4].start()
        kcopies[1].wait_recv()
        kacc[xp, two] += krelay_r[...]
        kcopies[5].start()

    def kjoined():
        for copy in kcopies[2:6]:
            copy.wait_recv()
        for i in range(2):
            kacc[x, pl.ds(2 * i, 2)] += kfrom_l[i] + kfrom_r[i]
        for copy in kcopies[6:]:
            copy.start()

    def kfinished():
        for copy in kcopies[6:]:
            copy.wait_recv()
        total = kacc[x, w] + kfrom_z[0] + kfrom_z[1] + kfrom_z[2]
        kout_ref[...] = total[0]
        vout_ref[...] = total[1]

    for t in range(pieces + 3):
        if t < pieces:
            mated(t)
        if t == 1:
            krelayed()
        if 0 <= t - 1 < pieces:
            relayed(t - 1)
        if t == pieces - 1:
            kjoined()
        if 0 <= t - 2 < pieces:
            joined(t - 2)
        if t == pieces + 1:
            kfinished()
        if 0 <= t - 3 < pieces:
            finished(t - 3)
    for p in range(pieces):
        for copy in copies[p]:
            copy.wait_send()
    for copy in kcopies:
        copy.wait_send()


def reduce(qp, kv, pieces):
    _, _, _, questions, part, width = qp.shape
    n = questions // pieces
    h = n // 2
    keys = kv.shape[3]
    f32 = jnp.float32
    anywhere, vmem = pl.BlockSpec(memory_space=pl.ANY), pl.BlockSpec(memory_space=pltpu.VMEM)
    return pl.pallas_call(
        partial(reduce_kernel, pieces),
        in_specs=[anywhere, anywhere],
        out_specs=[vmem] * 3,
        out_shape=[
            jax.ShapeDtypeStruct((questions, part, width), f32),
            jax.ShapeDtypeStruct((keys, width), f32),
            jax.ShapeDtypeStruct((keys, width), f32),
        ],
        scratch_shapes=[
            pltpu.VMEM((2, 4, questions, part, width), f32),
            pltpu.VMEM((2, 4, questions, part, width), f32),
            pltpu.VMEM((pieces, 2, h, part, width), f32),
            pltpu.VMEM((pieces, 2, h, part, width), f32),
            pltpu.VMEM((pieces, 2, 2, h, part, width), f32),
            pltpu.VMEM((pieces, 2, 2, h, part, width), f32),
            pltpu.VMEM((pieces, n, part, width), f32),
            pltpu.VMEM((4, 4, 2, keys, width), f32),
            pltpu.VMEM((2, 2, keys, width), f32),
            pltpu.VMEM((2, 2, keys, width), f32),
            pltpu.VMEM((2, 2, 2, keys, width), f32),
            pltpu.VMEM((2, 2, 2, keys, width), f32),
            pltpu.VMEM((3, 2, keys, width), f32),
            pltpu.SemaphoreType.DMA((pieces + 1,)),
            pltpu.SemaphoreType.DMA((pieces * 8,)),
            pltpu.SemaphoreType.DMA((pieces * 8,)),
            pltpu.SemaphoreType.DMA((9,)),
            pltpu.SemaphoreType.DMA((9,)),
        ],
        compiler_params=pltpu.CompilerParams(collective_id=0, has_side_effects=True),
        name="reduce",
    )(qp, kv)


PER_STEP = 4
PIECES = 4


def local(queries, keys, values, outputs_saved, grad_out, saved_lse, block_lists):
    questions, qlen, heads, width = queries.shape
    qg, kv = tiles(queries, keys, values, outputs_saved, grad_out, saved_lse, block_lists, 16, 16, PER_STEP)
    qg = qg.reshape(2, 2, 4, questions, qg.shape[2], width)
    kv = kv.reshape(4, 4, 2, kv.shape[2], width)
    query_grad, key_grad, value_grad = reduce(qg, kv, PIECES)
    return (query_grad.reshape(questions, -1, heads, width), key_grad, value_grad)


def solution(mesh):
    placed = (
        P("pb", None, None, None),
        P("ctx", None),
        P("ctx", None),
        P("pb", None, None, None),
        P("pb", None, None, None),
        P("pb", None, None),
        P("pb", None),
    )
    return jax.shard_map(
        local,
        mesh=mesh,
        in_specs=placed,
        out_specs=(P("pb", "ctx", None, None), P(("ctx", "pb"), None), P(("ctx", "pb"), None)),
        check_vma=False,
    )
```

time: 381 us -> 65.7 us (0.17)
  waiting for transfers between devices: 162 us -> 0 us
  matrix products: 143 us -> 0 us
  Pallas kernels: 0 us -> 57.9 us
  other arithmetic: 30.7 us -> 0 us
  local copies, waits for them, and re-layouts: 26 us -> 6.13 us
  between operations: 16.3 us -> 0.65 us
    dot_general x80 -> x0, matrix products: 143 us -> none  [the longest x16 33.1 us: question_step(): jnp.einsum('rk,rd->kd', prob_tile.astype(jnp.bfloat16), dout_rows, prefer...]
    unnamed x4 -> x0, waiting for transfers between devices: 106 us -> none
    pallas_call x0 -> x2, Pallas kernels: none -> 57.9 us  [the longest x1 37.6 us: reduce(): pl.pallas_call(partial(reduce_kernel, pieces), in_specs=[anywhere, anywhe...]
    reduce_scatter x2 -> x0, waiting for transfers between devices: 55.2 us -> none  [the longest x1 55.2 us: local(): lax.psum_scatter(value_acc.reshape(-1, head_width), 'pb', scatter_dimensi...]
    scatter-add x2 -> x0, other arithmetic: 25.9 us -> none  [the longest x1 13 us: local(): zero_acc.at[flat_chosen]]
    dynamic_slice x64 -> x0, local copies, waits for them, and re-layouts: 13 us -> none  [local(): lax.scan(stepper, 0, scanned)]
    gather x2 -> x0, local copies, waits for them, and re-layouts: 5.47 us -> none  [the longest x1 2.75 us: local(): value_blocks[chosen]]
  transfers between devices with their start and end apart: 3 -> 0, of which waited for: 2 -> 0; matrix products, arithmetic and copies ran while one was open for 8% -> 0% of each run, Pallas kernels for 0% -> 0%
where the time goes in v1:
time: 65.7 us; the launch traced here: 64.7 us
  Pallas kernels  57.9 us (88%)
  local copies, waits for them, and re-layouts  6.13 us (9%)
    pallas_call x1, Pallas kernels, reduce(): pl.pallas_call(partial(reduce_kernel, pieces), in_specs=[anywhere, anywhe...  37.6 us
    pallas_call x1, Pallas kernels, tiles(): pl.pallas_call(partial(tiles_kernel, per_step, rows), grid=(questions //...  20.3 us
    unnamed x4, local copies, waits for them, and re-layouts  5.41 us

profile of v1, /device:TPU:8, one launch (start us, length us, event | category | flops | bytes accessed | tf_op | source)
XLA Modules:
  0.0 64.7 jit_solution(1179975197544630549)
XLA Ops:
  0.6 1.0 %copy.11 = f32[16,64,8]{0,2,1:T(8,128)S(1)} copy(f32[16,64,8]{1,2,0:T(8,128)} %param.12) | data formatting | bytes 65536 | tf_op args[5]
  1.6 0.7 %copy.12.lse_ref = f32[16,1,512]{2,1,0:T(1,128)} copy(f32[16,1,512]{0,2,1:T(8,128)S(1)} %bitcast.12) | data formatting | bytes 65536 | tf_op jit(solution)/shard_map/reshape | solution.py:134
  2.3 20.3 %tiles.1 = (f32[16,16,32,128]{3,2,1,0:T(8,128)}, f32[16,2,64,128]{3,2,1,0:T(8,128)}) custom-call(s32[16,96]{1,0:T(8,128)} %lists_ref.1, bf16[16,512,128]{2,1,0:T(8,128)(2,1)} %bitcast.8, bf16[16,512,128]{2,1,0:T(8,128)(2,1)} %bitcast.9, bf16[16,512,128]{2,1,0:T(8,128)(2,1)} %bitcast.10, f32[16,1,512]{2,1,0:T(1,128)} %copy.12.lse_ref, ...), custom_call_target="tpu_custom_call" | custom-call | tf_op jit(solution)/shard_map/tiles/pallas_call | solution.py:109
  22.6 37.6 %reduce.1 = (f32[16,32,128]{2,1,0:T(8,128)}, f32[64,128]{1,0:T(8,128)}, f32[64,128]{1,0:T(8,128)}) custom-call(f32[2,2,4,16,32,128]{5,4,3,2,1,0:T(8,128)} %bitcast.7, f32[4,4,2,64,128]{4,3,2,1,0:T(8,128)} %bitcast.11), custom_call_target="tpu_custom_call" | custom-call | tf_op jit(solution)/shard_map/reduce/pallas_call | solution.py:288
  60.2 1.7 %copy.16 = f32[16,4,8,128]{3,2,1,0:T(8,128)} copy(f32[16,4,8,128]{3,2,1,0:T(8,128)} %bitcast.13) | data formatting | bytes 524288
  61.9 1.4 %copy.17 = f32[64,128]{1,0:T(8,128)} copy(f32[64,128]{1,0:T(8,128)} %get-tuple-element.17) | data formatting | bytes 65536
  63.3 1.4 %copy.18 = f32[64,128]{1,0:T(8,128)} copy(f32[64,128]{1,0:T(8,128)} %get-tuple-element.18) | data formatting | bytes 65536

commit v2 on v0

v2 whole, which is shorter than its diff:
```python
from functools import partial

import jax
import jax.numpy as jnp
from jax import lax
from jax.experimental import pallas as pl
from jax.experimental.pallas import tpu as pltpu
from jax.sharding import PartitionSpec as P

BLK = 128
CAP = 6
BLK_DEV = 8
D = 128
PIECES = 8
GROUP = 2
MESH = pl.DeviceIdType.MESH
LOG2E = 1.4426950408889634

NT = (((1,), (1,)), ((), ()))
NN = (((1,), (0,)), ((), ()))


def dot(a, b, dims):
    return lax.dot_general(a, b, dims, preferred_element_type=jnp.float32)


def slot_table(lists, first):
    questions = lists.shape[0]
    lane = lax.broadcasted_iota(jnp.int32, (questions, 128), 1)
    table = jnp.where(lane < 8, BLK_DEV, CAP)
    count = jnp.zeros((questions, 1), jnp.int32)
    for b in range(BLK_DEV):
        member = jnp.max(jnp.where(lists == first + b, 1, 0), axis=1, keepdims=True)
        table = jnp.where((member > 0) & (lane == count), b, table)
        table = jnp.where((member > 0) & (lane == 8 + b), count, table)
        count = count + member
    return table


def lse_lines(lse):
    questions, heads, tokens = lse.shape
    rows = tokens * heads
    flat = lse.reshape(questions * heads, tokens)
    high = flat.astype(jnp.bfloat16)
    rest = flat - high.astype(jnp.float32)
    mid = rest.astype(jnp.bfloat16)
    low = (rest - mid.astype(jnp.float32)).astype(jnp.bfloat16)
    token = lax.broadcasted_iota(jnp.int32, (tokens, rows), 0)
    column = lax.broadcasted_iota(jnp.int32, (tokens, rows), 1)
    spread = jnp.where(token == column // heads, 1.0, 0.0).astype(jnp.bfloat16)
    wide = dot(high, spread, NN) + dot(mid, spread, NN) + dot(low, spread, NN)
    wide = wide.reshape(questions, heads, rows)
    head = lax.broadcasted_iota(jnp.int32, (questions, heads, rows), 1)
    column = lax.broadcasted_iota(jnp.int32, (questions, heads, rows), 2)
    return jnp.sum(jnp.where(head == column % heads, wide, 0.0), axis=1, keepdims=True)


def fused_kernel(lists_ref, lse_ref, q_hbm, do_hbm, o_hbm, k_hbm, v_hbm, qout_ref, kvout_ref,
                 q_buf, do_buf, o_buf, kx, vx, ktx, lines, table_v, table, slots, kv,
                 qp, other, relay_l, relay_r, from_l, from_r, from_z,
                 krelay_l, krelay_r, kfrom_l, kfrom_r, kfrom_z,
                 load_sem, base_sem, send_sem, recv_sem, ksend_sem, krecv_sem):
    factor = D ** -0.5
    ctx, pb = lax.axis_index("ctx"), lax.axis_index("pb")
    c, y, z = ctx % 2, (ctx // 2) % 4, ctx // 8
    x, w = pb // 4, pb % 4
    yn, yp, yo = (y + 1) % 4, (y + 3) % 4, (y + 2) % 4
    xn, xp, xo = (x + 1) % 4, (x + 3) % 4, (x + 2) % 4
    at_ctx = lambda z_, y_, c_: {"ctx": z_ * 8 + y_ * 2 + c_}
    at_pb = lambda x_, w_: {"pb": x_ * 4 + w_}
    mate, right, left, across = at_ctx(z, y, 1 - c), at_ctx(z, yn, c), at_ctx(z, yp, c), at_ctx(1 - z, y, c)
    kright, kleft = at_pb(xn, w), at_pb(xp, w)
    kfar = [at_pb(x, (w + d) % 4) for d in (1, 2, 3)]
    n = q_buf.shape[0] // PIECES
    h = n // 2
    part = qp.shape[4]

    def loads(p):
        every = pl.ds(p * n, n)
        return [
            pltpu.make_async_copy(src.at[every], dst.at[every], load_sem.at[p, i])
            for i, (src, dst) in enumerate(((q_hbm, q_buf), (do_hbm, do_buf), (o_hbm, o_buf)))
        ]

    base = [
        pltpu.make_async_copy(k_hbm, kx.at[pl.ds(0, BLK_DEV)], base_sem.at[0]),
        pltpu.make_async_copy(v_hbm, vx.at[pl.ds(0, BLK_DEV)], base_sem.at[1]),
    ]
    for copy in base:
        copy.start()
    for p in range(PIECES):
        for copy in loads(p):
            copy.start()

    barrier = pltpu.get_barrier_semaphore()
    partners = [mate, right, left, across, kright, kleft] + kfar
    for device in partners:
        pl.semaphore_signal(barrier, inc=1, device_id=device, device_id_type=MESH)

    table_v[...] = slot_table(lists_ref[...], ctx * BLK_DEV)
    move = pltpu.make_async_copy(table_v, table, base_sem.at[2])
    move.start()
    lines[...] = lse_lines(lse_ref[...]) * LOG2E
    kv[...] = jnp.zeros_like(kv)
    slots[...] = jnp.zeros_like(slots)
    for ref in (kx, vx, ktx):
        ref[BLK_DEV] = jnp.zeros_like(ref[BLK_DEV])
    for copy in base:
        copy.wait()
    for b in range(BLK_DEV):
        ktx[b] = kx[b].T
    move.wait()
    pl.semaphore_wait(barrier, len(partners))

    def remote(src, dst, send, recv, device):
        return pltpu.make_async_remote_copy(
            src_ref=src, dst_ref=dst, send_sem=send, recv_sem=recv,
            device_id=device, device_id_type=MESH)

    def copies(p):
        every, one, two = pl.ds(p * n, n), pl.ds(p * n, h), pl.ds(p * n + h, h)
        make = lambda k, src, dst, device: remote(src, dst, send_sem.at[p, k], recv_sem.at[p, k], device)
        return [
            make(0, qp.at[1 - c, :, :, every], other.at[:, :, every], mate),
            make(1, qp.at[c, :, yo, one], relay_l.at[p], right),
            make(2, qp.at[c, :, yo, two], relay_r.at[p], left),
            make(3, qp.at[c, :, yn, two], from_l.at[p, 1], right),
            make(4, qp.at[c, :, yp, one], from_r.at[p, 0], left),
            make(5, qp.at[c, :, yn, one], from_l.at[p, 0], right),
            make(6, qp.at[c, :, yp, two], from_r.at[p, 1], left),
            make(7, qp.at[c, 1 - z, y, every], from_z.at[p], across),
        ]

    def kcopies(g):
        one, two = pl.ds(0, 2), pl.ds(2, 2)
        make = lambda k, src, dst, device: remote(src, dst, ksend_sem.at[g, k], krecv_sem.at[g, k], device)
        return [
            make(0, kv.at[g, xo, one], krelay_l.at[g], kright),
            make(1, kv.at[g, xo, two], krelay_r.at[g], kleft),
            make(2, kv.at[g, xn, two], kfrom_l.at[g, 1], kright),
            make(3, kv.at[g, xp, one], kfrom_r.at[g, 0], kleft),
            make(4, kv.at[g, xn, one], kfrom_l.at[g, 0], kright),
            make(5, kv.at[g, xp, two], kfrom_r.at[g, 1], kleft),
        ] + [make(6 + i, kv.at[g, x, (w + i + 1) % 4], kfrom_z.at[g, i], kfar[i]) for i in range(3)]

    def mated(p):
        every = pl.ds(p * n, n)
        todo = copies(p)
        todo[0].wait_recv()
        qp[c, :, :, every] += other[:, :, every]
        for copy in todo[1:5]:
            copy.start()

    def relayed(p):
        one, two = pl.ds(p * n, h), pl.ds(p * n + h, h)
        todo = copies(p)
        todo[1].wait_recv()
        qp[c, :, yn, one] += relay_l[p]
        todo[5].start()
        todo[2].wait_recv()
        qp[c, :, yp, two] += relay_r[p]
        todo[6].start()

    def joined(p):
        todo = copies(p)
        for copy in todo[3:7]:
            copy.wait_recv()
        for i in range(2):
            half = pl.ds(p * n + i * h, h)
            qp[c, :, y, half] += from_l[p, i] + from_r[p, i]
        todo[7].start()

    def finished(p):
        every = pl.ds(p * n, n)
        copies(p)[7].wait_recv()
        qout_ref[every] = qp[c, z, y, every] + from_z[p]

    def kstart(g):
        for copy in kcopies(g)[:4]:
            copy.start()

    def krelayed(g):
        todo = kcopies(g)
        todo[0].wait_recv()
        kv[g, xn, pl.ds(0, 2)] += krelay_l[g]
        todo[4].start()
        todo[1].wait_recv()
        kv[g, xp, pl.ds(2, 2)] += krelay_r[g]
        todo[5].start()

    def kjoined(g):
        todo = kcopies(g)
        for copy in todo[2:6]:
            copy.wait_recv()
        for i in range(2):
            kv[g, x, pl.ds(2 * i, 2)] += kfrom_l[g, i] + kfrom_r[g, i]
        for copy in todo[6:]:
            copy.start()

    def kfinished(g):
        for copy in kcopies(g)[6:]:
            copy.wait_recv()
        kvout_ref[g] = kv[g, x, w] + kfrom_z[g, 0] + kfrom_z[g, 1] + kfrom_z[g, 2]

    ones = jnp.ones((8, 2 * D), jnp.bfloat16)

    def gather_slots(row, side):
        for b in range(BLK_DEV):
            slot = table[row, 8 + b]
            for g in range(2):
                at = (g, b // 2, pl.ds((2 * b) % 4, 2))
                kv[at] += slots[side, slot, g].reshape(2, BLK // 2, D)

    def question(row, side):
        gather_slots(jnp.maximum(row - 1, 0), 1 - side)
        q, do = q_buf[row], do_buf[row]
        prod = do.astype(jnp.float32) * o_buf[row].astype(jnp.float32)
        high = prod.astype(jnp.bfloat16)
        low = (prod - high.astype(jnp.float32)).astype(jnp.bfloat16)
        delta = dot(ones, jnp.concatenate([high, low], axis=1), NT)[0:1]
        line = lines[row]
        blocks = [table[row, s] for s in range(CAP)]
        dscores = []
        for j in range(0, CAP, GROUP):
            some = blocks[j:j + GROUP]
            kb = jnp.concatenate([kx[b] for b in some], axis=0)
            vb = jnp.concatenate([vx[b] for b in some], axis=0)
            prob = jnp.exp2(dot(kb, q, NT) * (factor * LOG2E) - line)
            dscore = (prob * (dot(vb, do, NT) - delta)).astype(jnp.bfloat16)
            value_part = dot(prob.astype(jnp.bfloat16), do, NN)
            key_part = dot(dscore, q, NN)
            dscores.append(dscore)
            for i in range(GROUP):
                slots[side, j + i, 0] = key_part[i * BLK:(i + 1) * BLK]
                slots[side, j + i, 1] = value_part[i * BLK:(i + 1) * BLK]
        kt = jnp.concatenate([ktx[b] for b in blocks], axis=1)
        grad = dot(kt, jnp.concatenate(dscores, axis=0), NN).T * factor
        for s in range(16):
            qp[s % 2, s // 8, (s // 2) % 4, row] = grad[s * part:(s + 1) * part]

    def piece(p, _):
        for copy in loads(p):
            copy.wait()
        for i in range(n):
            question(p * n + i, i % 2)
        copies(p)[0].start()
        for lag, stage in ((4, finished), (3, joined), (2, relayed), (1, mated)):
            @pl.when(p >= lag)
            def _():
                stage(p - lag)
        return 0

    lax.fori_loop(0, PIECES, piece, 0)
    last = PIECES - 1
    gather_slots(PIECES * n - 1, (n - 1) % 2)
    kstart(1)
    kv[0] = kv[0] * factor
    kstart(0)
    mated(last)
    relayed(last - 1)
    joined(last - 2)
    finished(last - 3)
    krelayed(1)
    relayed(last)
    krelayed(0)
    joined(last - 1)
    finished(last - 2)
    kjoined(1)
    joined(last)
    finished(last - 1)
    kjoined(0)
    finished(last)
    kfinished(1)
    kfinished(0)

    def sent(p, _):
        for copy in copies(p):
            copy.wait_send()
        return 0

    lax.fori_loop(0, PIECES, sent, 0)
    for g in range(2):
        for copy in kcopies(g):
            copy.wait_send()


def fused(queries, keys, values, outputs_saved, grad_out, saved_lse, block_lists):
    questions, qlen, heads, width = queries.shape
    rows = qlen * heads
    part = rows // 16
    n = questions // PIECES
    h = n // 2
    cut = keys.shape[0] // 16
    f32, bf16 = jnp.float32, jnp.bfloat16
    flat = lambda a: a.reshape(questions, rows, width)
    blocks = lambda a: a.reshape(BLK_DEV, BLK, width)
    anywhere, vmem = pl.BlockSpec(memory_space=pl.ANY), pl.BlockSpec(memory_space=pltpu.VMEM)
    return pl.pallas_call(
        fused_kernel,
        in_specs=[vmem, vmem] + [anywhere] * 5,
        out_specs=[vmem] * 2,
        out_shape=[
            jax.ShapeDtypeStruct((questions, part, width), f32),
            jax.ShapeDtypeStruct((2, cut, width), f32),
        ],
        scratch_shapes=[
            pltpu.VMEM((questions, rows, width), bf16),
            pltpu.VMEM((questions, rows, width), bf16),
            pltpu.VMEM((questions, rows, width), bf16),
            pltpu.VMEM((BLK_DEV + 1, BLK, width), bf16),
            pltpu.VMEM((BLK_DEV + 1, BLK, width), bf16),
            pltpu.VMEM((BLK_DEV + 1, width, BLK), bf16),
            pltpu.VMEM((questions, 1, rows), f32),
            pltpu.VMEM((questions, 128), jnp.int32),
            pltpu.SMEM((questions, 128), jnp.int32),
            pltpu.VMEM((2, CAP + 1, 2, BLK, width), f32),
            pltpu.VMEM((2, 4, 4, cut, width), f32),
            pltpu.VMEM((2, 2, 4, questions, part, width), f32),
            pltpu.VMEM((2, 4, questions, part, width), f32),
            pltpu.VMEM((PIECES, 2, h, part, width), f32),
            pltpu.VMEM((PIECES, 2, h, part, width), f32),
            pltpu.VMEM((PIECES, 2, 2, h, part, width), f32),
            pltpu.VMEM((PIECES, 2, 2, h, part, width), f32),
            pltpu.VMEM((PIECES, n, part, width), f32),
            pltpu.VMEM((2, 2, cut, width), f32),
            pltpu.VMEM((2, 2, cut, width), f32),
            pltpu.VMEM((2, 2, 2, cut, width), f32),
            pltpu.VMEM((2, 2, 2, cut, width), f32),
            pltpu.VMEM((2, 3, cut, width), f32),
            pltpu.SemaphoreType.DMA((PIECES, 3)),
            pltpu.SemaphoreType.DMA((3,)),
            pltpu.SemaphoreType.DMA((PIECES, 8)),
            pltpu.SemaphoreType.DMA((PIECES, 8)),
            pltpu.SemaphoreType.DMA((2, 9)),
            pltpu.SemaphoreType.DMA((2, 9)),
        ],
        compiler_params=pltpu.CompilerParams(collective_id=0, has_side_effects=True),
        name="fused",
    )(block_lists, saved_lse.transpose(0, 2, 1), flat(queries), flat(grad_out), flat(outputs_saved),
      blocks(keys), blocks(values))


def spread_kernel(q_ref, kv_ref, qout_ref, kout_ref, vout_ref):
    qout_ref[...] = q_ref[...]
    kout_ref[...] = kv_ref[0]
    vout_ref[...] = kv_ref[1]


def local(queries, keys, values, outputs_saved, grad_out, saved_lse, block_lists):
    questions, qlen, heads, width = queries.shape
    query_grad, both = fused(queries, keys, values, outputs_saved, grad_out, saved_lse, block_lists)
    vmem = pl.BlockSpec(memory_space=pltpu.VMEM)
    query_grad, key_grad, value_grad = pl.pallas_call(
        spread_kernel,
        in_specs=[vmem] * 2,
        out_specs=[vmem] * 3,
        out_shape=[jax.ShapeDtypeStruct(s, jnp.float32) for s in (query_grad.shape, both.shape[1:], both.shape[1:])],
        name="spread",
    )(query_grad, both)
    return (query_grad.reshape(questions, -1, heads, width), key_grad, value_grad)


def solution(mesh):
    placed = (
        P("pb", None, None, None),
        P("ctx", None),
        P("ctx", None),
        P("pb", None, None, None),
        P("pb", None, None, None),
        P("pb", None, None),
        P("pb", None),
    )
    return jax.shard_map(
        local,
        mesh=mesh,
        in_specs=placed,
        out_specs=(P("pb", "ctx", None, None), P(("ctx", "pb"), None), P(("ctx", "pb"), None)),
        check_vma=False,
    )
```

time: 381 us -> 58.7 us (0.15)
  waiting for transfers between devices: 162 us -> 0 us
  matrix products: 143 us -> 0 us
  Pallas kernels: 0 us -> 57.9 us
  other arithmetic: 30.7 us -> 0 us
  local copies, waits for them, and re-layouts: 26 us -> 0 us
  between operations: 16.3 us -> 0.64 us
    dot_general x80 -> x0, matrix products: 143 us -> none  [the longest x16 33.1 us: question_step(): jnp.einsum('rk,rd->kd', prob_tile.astype(jnp.bfloat16), dout_rows, prefer...]
    unnamed x4 -> x0, waiting for transfers between devices: 106 us -> none
    pallas_call x0 -> x2, Pallas kernels: none -> 57.9 us  [the longest x1 56.2 us: fused(): pl.pallas_call(fused_kernel, in_specs=[vmem, vmem] + [anywhere] * 5, out_...]
    reduce_scatter x2 -> x0, waiting for transfers between devices: 55.2 us -> none  [the longest x1 55.2 us: local(): lax.psum_scatter(value_acc.reshape(-1, head_width), 'pb', scatter_dimensi...]
    scatter-add x2 -> x0, other arithmetic: 25.9 us -> none  [the longest x1 13 us: local(): zero_acc.at[flat_chosen]]
    dynamic_slice x64 -> x0, local copies, waits for them, and re-layouts: 13 us -> none  [local(): lax.scan(stepper, 0, scanned)]
    gather x2 -> x0, local copies, waits for them, and re-layouts: 5.47 us -> none  [the longest x1 2.75 us: local(): value_blocks[chosen]]
    unnamed x15 -> x0, local copies, waits for them, and re-layouts: 3.88 us -> none
  transfers between devices with their start and end apart: 3 -> 0, of which waited for: 2 -> 0; matrix products, arithmetic and copies ran while one was open for 8% -> 0% of each run, Pallas kernels for 0% -> 0%
where the time goes in v2:
time: 58.7 us; the launch traced here: 58.5 us
  Pallas kernels  57.9 us (99%)
  between operations  0.64 us (1%)
    pallas_call x1, Pallas kernels, fused(): pl.pallas_call(fused_kernel, in_specs=[vmem, vmem] + [anywhere] * 5, out_...  56.2 us
    pallas_call x1, Pallas kernels, local(): pl.pallas_call(spread_kernel, in_specs=[vmem] * 2, out_specs=[vmem] * 3,...  1.68 us

profile of v2, /device:TPU:8, one launch (start us, length us, event | category | flops | bytes accessed | tf_op | source)
XLA Modules:
  0.0 58.5 jit_solution(763996750889542143)
XLA Ops:
  0.6 56.2 %fused.1 = (f32[16,32,128]{2,1,0:T(8,128)}, f32[2,64,128]{2,1,0:T(8,128)}) custom-call(s32[16,96]{1,0:T(8,128)} %lists_ref.1, f32[16,8,64]{2,1,0:T(8,128)} %bitcast.12, bf16[16,512,128]{2,1,0:T(8,128)(2,1)} %bitcast.7, bf16[16,512,128]{2,1,0:T(8,128)(2,1)} %bitcast.8, bf16[16,512,128]{2,1,0:T(8,128)(2,1)} %bitcast.9, bf16[8,128,128]{2,1,0:T(8,128)(2,1)} %bitcast.10, ...), custom_call_target="tpu_custom_call" | custom-call | tf_op jit(solution)/shard_map/fused/pallas_call | solution.py:298
  56.8 1.7 %spread.1 = (f32[16,32,128]{2,1,0:T(8,128)}, f32[64,128]{1,0:T(8,128)}, f32[64,128]{1,0:T(8,128)}) custom-call(f32[16,32,128]{2,1,0:T(8,128)} %get-tuple-element.8.q_ref, f32[2,64,128]{2,1,0:T(8,128)} %get-tuple-element.9.kv_ref), custom_call_target="tpu_custom_call" | custom-call | tf_op jit(solution)/shard_map/spread/pallas_call | solution.py:353

commit v3 on v2

--- a/solution.py
+++ b/solution.py
@@ -12,7 +12,6 @@
 BLK_DEV = 8
 D = 128
 PIECES = 8
-GROUP = 2
 MESH = pl.DeviceIdType.MESH
 LOG2E = 1.4426950408889634
 
@@ -56,7 +55,7 @@
 
 
 def fused_kernel(lists_ref, lse_ref, q_hbm, do_hbm, o_hbm, k_hbm, v_hbm, qout_ref, kvout_ref,
-                 q_buf, do_buf, o_buf, kx, vx, ktx, lines, table_v, table, slots, kv,
+                 q_buf, do_buf, o_buf, kx, vx, ktx, lines, table_v, table, slots, kvt, kv,
                  qp, other, relay_l, relay_r, from_l, from_r, from_z,
                  krelay_l, krelay_r, kfrom_l, kfrom_r, kfrom_z,
                  load_sem, base_sem, send_sem, recv_sem, ksend_sem, krecv_sem):
@@ -101,7 +100,7 @@
     move = pltpu.make_async_copy(table_v, table, base_sem.at[2])
     move.start()
     lines[...] = lse_lines(lse_ref[...]) * LOG2E
-    kv[...] = jnp.zeros_like(kv)
+    kvt[...] = jnp.zeros_like(kvt)
     slots[...] = jnp.zeros_like(slots)
     for ref in (kx, vx, ktx):
         ref[BLK_DEV] = jnp.zeros_like(ref[BLK_DEV])
@@ -119,7 +118,7 @@
 
     def copies(p):
         every, one, two = pl.ds(p * n, n), pl.ds(p * n, h), pl.ds(p * n + h, h)
-        make = lambda k, src, dst, device: remote(src, dst, send_sem.at[p, k], recv_sem.at[p, k], device)
+        make = lambda k, src, dst, device: lambda: remote(src, dst, send_sem.at[p, k], recv_sem.at[p, k], device)
         return [
             make(0, qp.at[1 - c, :, :, every], other.at[:, :, every], mate),
             make(1, qp.at[c, :, yo, one], relay_l.at[p], right),
@@ -133,7 +132,7 @@
 
     def kcopies(g):
         one, two = pl.ds(0, 2), pl.ds(2, 2)
-        make = lambda k, src, dst, device: remote(src, dst, ksend_sem.at[g, k], krecv_sem.at[g, k], device)
+        make = lambda k, src, dst, device: lambda: remote(src, dst, ksend_sem.at[g, k], krecv_sem.at[g, k], device)
         return [
             make(0, kv.at[g, xo, one], krelay_l.at[g], kright),
             make(1, kv.at[g, xo, two], krelay_r.at[g], kleft),
@@ -146,104 +145,104 @@
     def mated(p):
         every = pl.ds(p * n, n)
         todo = copies(p)
-        todo[0].wait_recv()
+        todo[0]().wait_recv()
         qp[c, :, :, every] += other[:, :, every]
         for copy in todo[1:5]:
-            copy.start()
+            copy().start()
 
     def relayed(p):
         one, two = pl.ds(p * n, h), pl.ds(p * n + h, h)
         todo = copies(p)
-        todo[1].wait_recv()
+        todo[1]().wait_recv()
         qp[c, :, yn, one] += relay_l[p]
-        todo[5].start()
-        todo[2].wait_recv()
+        todo[5]().start()
+        todo[2]().wait_recv()
         qp[c, :, yp, two] += relay_r[p]
-        todo[6].start()
+        todo[6]().start()
 
     def joined(p):
         todo = copies(p)
         for copy in todo[3:7]:
-            copy.wait_recv()
+            copy().wait_recv()
         for i in range(2):
             half = pl.ds(p * n + i * h, h)
             qp[c, :, y, half] += from_l[p, i] + from_r[p, i]
-        todo[7].start()
+        todo[7]().start()
 
     def finished(p):
         every = pl.ds(p * n, n)
-        copies(p)[7].wait_recv()
+        copies(p)[7]().wait_recv()
         qout_ref[every] = qp[c, z, y, every] + from_z[p]
-
-    def kstart(g):
-        for copy in kcopies(g)[:4]:
-            copy.start()
 
     def krelayed(g):
         todo = kcopies(g)
-        todo[0].wait_recv()
+        todo[0]().wait_recv()
         kv[g, xn, pl.ds(0, 2)] += krelay_l[g]
-        todo[4].start()
-        todo[1].wait_recv()
+        todo[4]().start()
+        todo[1]().wait_recv()
         kv[g, xp, pl.ds(2, 2)] += krelay_r[g]
-        todo[5].start()
+        todo[5]().start()
 
     def kjoined(g):
         todo = kcopies(g)
         for copy in todo[2:6]:
-            copy.wait_recv()
+            copy().wait_recv()
         for i in range(2):
             kv[g, x, pl.ds(2 * i, 2)] += kfrom_l[g, i] + kfrom_r[g, i]
         for copy in todo[6:]:
-            copy.start()
+            copy().start()
 
     def kfinished(g):
         for copy in kcopies(g)[6:]:
-            copy.wait_recv()
+            copy().wait_recv()
         kvout_ref[g] = kv[g, x, w] + kfrom_z[g, 0] + kfrom_z[g, 1] + kfrom_z[g, 2]
 
     ones = jnp.ones((8, 2 * D), jnp.bfloat16)
 
-    def gather_slots(row, side):
+    def gather_slots(rows):
         for b in range(BLK_DEV):
-            slot = table[row, 8 + b]
+            at = [table[row, 8 + b] for row in rows]
             for g in range(2):
-                at = (g, b // 2, pl.ds((2 * b) % 4, 2))
-                kv[at] += slots[side, slot, g].reshape(2, BLK // 2, D)
-
-    def question(row, side):
-        gather_slots(jnp.maximum(row - 1, 0), 1 - side)
+                kvt[g, b] += sum(slots[side, slot, g] for side, slot in enumerate(at))
+
+    def flush(strip):
+        for g in range(2):
+            for i in range(2):
+                block = kvt[g, 2 * strip + i].T
+                block = block * factor if g == 0 else block
+                kv[g, strip, pl.ds(2 * i, 2)] = block.reshape(2, BLK // 2, D)
+
+    def scores_of(row):
         q, do = q_buf[row], do_buf[row]
+        blocks = [table[row, s] for s in range(CAP)]
         prod = do.astype(jnp.float32) * o_buf[row].astype(jnp.float32)
         high = prod.astype(jnp.bfloat16)
         low = (prod - high.astype(jnp.float32)).astype(jnp.bfloat16)
         delta = dot(ones, jnp.concatenate([high, low], axis=1), NT)[0:1]
-        line = lines[row]
-        blocks = [table[row, s] for s in range(CAP)]
-        dscores = []
-        for j in range(0, CAP, GROUP):
-            some = blocks[j:j + GROUP]
-            kb = jnp.concatenate([kx[b] for b in some], axis=0)
-            vb = jnp.concatenate([vx[b] for b in some], axis=0)
-            prob = jnp.exp2(dot(kb, q, NT) * (factor * LOG2E) - line)
-            dscore = (prob * (dot(vb, do, NT) - delta)).astype(jnp.bfloat16)
-            value_part = dot(prob.astype(jnp.bfloat16), do, NN)
-            key_part = dot(dscore, q, NN)
-            dscores.append(dscore)
-            for i in range(GROUP):
-                slots[side, j + i, 0] = key_part[i * BLK:(i + 1) * BLK]
-                slots[side, j + i, 1] = value_part[i * BLK:(i + 1) * BLK]
-        kt = jnp.concatenate([ktx[b] for b in blocks], axis=1)
-        grad = dot(kt, jnp.concatenate(dscores, axis=0), NN).T * factor
+        kb = jnp.concatenate([kx[b] for b in blocks], axis=0)
+        vb = jnp.concatenate([vx[b] for b in blocks], axis=0)
+        prob = jnp.exp2(dot(kb, q, NT) * (factor * LOG2E) - lines[row])
+        dscore = (prob * (dot(vb, do, NT) - delta)).astype(jnp.bfloat16)
+        return prob.astype(jnp.bfloat16), dscore
+
+    def sums_of(row, side, prob, dscore):
+        value_part = dot(do_buf[row].T, prob, NT)
+        key_part = dot(q_buf[row].T, dscore, NT)
+        for s in range(CAP):
+            slots[side, s, 0] = key_part[:, s * BLK:(s + 1) * BLK]
+            slots[side, s, 1] = value_part[:, s * BLK:(s + 1) * BLK]
+        kt = jnp.concatenate([ktx[table[row, s]] for s in range(CAP)], axis=1)
+        grad = dot(kt, dscore, NN).T * factor
         for s in range(16):
             qp[s % 2, s // 8, (s // 2) % 4, row] = grad[s * part:(s + 1) * part]
 
     def piece(p, _):
         for copy in loads(p):
             copy.wait()
+        gather_slots([jnp.maximum(p - 1, 0) * n + i for i in range(n)])
         for i in range(n):
-            question(p * n + i, i % 2)
-        copies(p)[0].start()
+            sums_of(p * n + i, i, *scores_of(p * n + i))
+        copies(p)[0]().start()
         for lag, stage in ((4, finished), (3, joined), (2, relayed), (1, mated)):
             @pl.when(p >= lag)
             def _():
@@ -252,10 +251,12 @@
 
     lax.fori_loop(0, PIECES, piece, 0)
     last = PIECES - 1
-    gather_slots(PIECES * n - 1, (n - 1) % 2)
-    kstart(1)
-    kv[0] = kv[0] * factor
-    kstart(0)
+    gather_slots([last * n + i for i in range(n)])
+    for strip, starts in ((xo, (0, 1)), (xn, (2,)), (xp, (3,)), (x, ())):
+        flush(strip)
+        for g in (1, 0):
+            for k in starts:
+                kcopies(g)[k]().start()
     mated(last)
     relayed(last - 1)
     joined(last - 2)
@@ -275,13 +276,13 @@
 
     def sent(p, _):
         for copy in copies(p):
-            copy.wait_send()
+            copy().wait_send()
         return 0
 
     lax.fori_loop(0, PIECES, sent, 0)
     for g in range(2):
         for copy in kcopies(g):
-            copy.wait_send()
+            copy().wait_send()
 
 
 def fused(queries, keys, values, outputs_saved, grad_out, saved_lse, block_lists):
@@ -313,7 +314,8 @@
             pltpu.VMEM((questions, 1, rows), f32),
             pltpu.VMEM((questions, 128), jnp.int32),
             pltpu.SMEM((questions, 128), jnp.int32),
-            pltpu.VMEM((2, CAP + 1, 2, BLK, width), f32),
+            pltpu.VMEM((n, CAP + 1, 2, width, BLK), f32),
+            pltpu.VMEM((2, BLK_DEV, width, BLK), f32),
             pltpu.VMEM((2, 4, 4, cut, width), f32),
             pltpu.VMEM((2, 2, 4, questions, part, width), f32),
             pltpu.VMEM((2, 4, questions, part, width), f32),

time: 58.7 us -> 59.1 us (level)
  no operation moved by 1% of the time
where the time goes in v3:
time: 59.1 us; the launch traced here: 58.8 us
  Pallas kernels  58.2 us (98%)
  between operations  0.64 us (1%)
    pallas_call x1, Pallas kernels, fused(): pl.pallas_call(fused_kernel, in_specs=[vmem, vmem] + [anywhere] * 5, out_...  56.5 us
    pallas_call x1, Pallas kernels, local(): pl.pallas_call(spread_kernel, in_specs=[vmem] * 2, out_specs=[vmem] * 3,...  1.68 us

profile of v3, /device:TPU:8, one launch (start us, length us, event | category | flops | bytes accessed | tf_op | source)
XLA Modules:
  0.0 58.8 jit_solution(4852442230622952868)
XLA Ops:
  0.6 56.5 %fused.1 = (f32[16,32,128]{2,1,0:T(8,128)}, f32[2,64,128]{2,1,0:T(8,128)}) custom-call(s32[16,96]{1,0:T(8,128)} %lists_ref.1, f32[16,8,64]{2,1,0:T(8,128)} %bitcast.12, bf16[16,512,128]{2,1,0:T(8,128)(2,1)} %bitcast.7, bf16[16,512,128]{2,1,0:T(8,128)(2,1)} %bitcast.8, bf16[16,512,128]{2,1,0:T(8,128)(2,1)} %bitcast.9, bf16[8,128,128]{2,1,0:T(8,128)(2,1)} %bitcast.10, ...), custom_call_target="tpu_custom_call" | custom-call | tf_op jit(solution)/shard_map/fused/pallas_call | solution.py:299
  57.2 1.7 %spread.1 = (f32[16,32,128]{2,1,0:T(8,128)}, f32[64,128]{1,0:T(8,128)}, f32[64,128]{1,0:T(8,128)}) custom-call(f32[16,32,128]{2,1,0:T(8,128)} %get-tuple-element.8.q_ref, f32[2,64,128]{2,1,0:T(8,128)} %get-tuple-element.9.kv_ref), custom_call_target="tpu_custom_call" | custom-call | tf_op jit(solution)/shard_map/spread/pallas_call | solution.py:355
